TPU v7x, 256 devices: a whole 4x4x8 slice. The times are simulated.
256 devices in a mesh: tile: 128 (over y, z, x), sub: 2 (over core).
Axes of the slice: x: 4, y: 4, z: 8, core: 2. Of those that a mesh axis runs over, the one named last changes fastest.
Arguments:
- right_side: float32 [2, 32768, 256], P(None, ('tile', 'sub')), may hold values from -12 to 12
- pixel_weight: float32 [32768, 256], P(('tile', 'sub')), may hold values from 0.5 to 2
- noise_diag: float32 [2, 32768, 256], P(None, ('tile', 'sub')), may hold values from 0.5 to 8
- noise_corr: float32 [32768, 256], P(('tile', 'sub')), may hold values from -0.8 to 0.8
- neighbours: int32 [3, 4, 128], replicated, may hold values from 0 to 127, as said below
Outputs:
- solution: float32 [2, 32768, 256], P(None, ('tile', 'sub'))
- final_misfit: float32 [2, 32768, 256], P(None, ('tile', 'sub'))
Inputs may be any that keep to these rules, and one draw needn't show every extreme that they name: `neighbours`: across side 0 lies side 1 of another or the same tile and across side 2 lies side 3, and conversely; the relation is symmetric, with the same reversal flag on both sides of an edge. Every neighbour lies, in the cyclic order of tiles, within 3 places of its tile or within 3 places of the tile 128/2 places away, and 3 places is reached. Flags are 0 or 1.
All inputs are finite; a program needn't handle non-finite values.
Results may differ from a plain program's by a relative error of at most 0.00012.
Values sent between devices are 32-bit elements; how exact they have to be, the bound alone decides.
A program may use at most 128 MiB of HBM per device.

v0:
```python
import jax
import jax.numpy as jnp
from jax import lax
from jax.sharding import PartitionSpec as P

NU = 2
NC = 3


MASS = 0.05
OMEGA = 0.8


def with_halo(block, sides, width):
    for axis, dim in sides:
        count = lax.axis_size(axis)
        forward = [(i, i + 1) for i in range(count - 1)]
        backward = [(target, source) for source, target in forward]
        low = lax.ppermute(
            lax.slice_in_dim(block, block.shape[dim] - width, None, axis=dim), axis, forward
        )
        high = lax.ppermute(lax.slice_in_dim(block, 0, width, axis=dim), axis, backward)
        block = jnp.concatenate([low, block, high], axis=dim)
    return block


def inverse_blocks(diag_term, noise_terms):
    upper_left = diag_term + noise_terms[0]
    lower_right = diag_term + noise_terms[1]
    determinant = upper_left * lower_right - noise_terms[2] * noise_terms[2]
    return jnp.stack(
        [lower_right / determinant, upper_left / determinant, -noise_terms[2] / determinant]
    )


def apply_block(inverse, misfit):
    out_first = inverse[0] * misfit[0] + inverse[2] * misfit[1]
    second = inverse[2] * misfit[0] + inverse[1] * misfit[1]
    return jnp.stack([out_first, second])


def coarsen_sum(values):
    old_shape = values.shape
    new_shape = old_shape[:-2] + (old_shape[-2] // 2, 2, old_shape[-1] // 2, 2)
    return values.reshape(new_shape).sum(axis=(-3, -1))


def prolong(values):
    return jnp.repeat(jnp.repeat(values, 2, axis=-2), 2, axis=-1)


def across_sides(side_rows, link_cols, grid_level):
    if grid_level == "fine":
        everyone = lax.all_gather(side_rows[None], "tile", axis=0, tiled=True)
    else:
        everyone = lax.all_gather(side_rows[None], "tile", axis=0, tiled=True)
    across = everyone[link_cols[0], link_cols[1]]
    flipped = jnp.flip(across, axis=2)
    return jnp.where(link_cols[2][:, None, None] == 1, flipped, across)


def band_sum(scaled, link_cols, grid_level):
    sub_id = lax.axis_index("sub")
    sub_count = lax.axis_size("sub")
    band_rows = scaled.shape[1]
    band_width = scaled.shape[2]
    if grid_level == "fine":
        padded = with_halo(scaled, (("sub", 1),), 1)
    else:
        padded = with_halo(scaled, (("sub", 1),), 1)
    zeros_row = jnp.zeros((2, band_width), jnp.float32)
    start_row = (jnp.int32(0), sub_id * band_rows)
    top_part = jnp.where(sub_id == 0, scaled[:, 0, :], zeros_row)
    bottom_part = jnp.where(sub_id == sub_count - 1, scaled[:, band_rows - 1, :], zeros_row)
    left_part = lax.dynamic_update_slice(zeros_row, scaled[:, :, 0], start_row)
    right_part = lax.dynamic_update_slice(zeros_row, scaled[:, :, band_width - 1], start_row)
    partial_sides = jnp.stack([top_part, bottom_part, left_part, right_part])
    if grid_level == "fine":
        side_rows = lax.psum(partial_sides, "sub")
    else:
        side_rows = lax.psum(partial_sides, "sub")
    across = across_sides(side_rows, link_cols, grid_level)
    upper_row = padded[:, 0, :] + jnp.where(sub_id == 0, across[0], zeros_row)
    lower_row = padded[:, band_rows + 1, :] + jnp.where(
        sub_id == sub_count - 1, across[1], zeros_row
    )
    left_col = lax.dynamic_slice(across[2], start_row, (2, band_rows))
    right_col = lax.dynamic_slice(across[3], start_row, (2, band_rows))
    above_rows = jnp.concatenate([upper_row[:, None, :], scaled[:, :-1, :]], axis=1)
    below_rows = jnp.concatenate([scaled[:, 1:, :], lower_row[:, None, :]], axis=1)
    west_cols = jnp.concatenate([left_col[:, :, None], scaled[:, :, :-1]], axis=2)
    east_cols = jnp.concatenate([scaled[:, :, 1:], right_col[:, :, None]], axis=2)
    return above_rows + below_rows + west_cols + east_cols


def operate(iterate, weight, stiffness, noise_terms, link_cols, grid_level):
    scaled = weight * iterate
    beside_all = band_sum(scaled, link_cols, grid_level)
    stencil = (MASS + 4.0) * scaled - beside_all
    out_first = (
        stiffness * weight * stencil[0] + noise_terms[0] * iterate[0] + noise_terms[2] * iterate[1]
    )
    second = (
        stiffness * weight * stencil[1] + noise_terms[2] * iterate[0] + noise_terms[1] * iterate[1]
    )
    return jnp.stack([out_first, second])


def relax(iterate, source, weight, stiffness, noise_terms, inverse, link_cols, grid_level):
    misfit = source - operate(iterate, weight, stiffness, noise_terms, link_cols, grid_level)
    return iterate + OMEGA * apply_block(inverse, misfit)


def coarse_solve(coarse_source, coarse_weight, coarse_noise, link_cols):
    coarse_inverse = inverse_blocks(
        2.0 * (MASS + 4.0) * coarse_weight * coarse_weight, coarse_noise
    )
    correction = OMEGA * apply_block(coarse_inverse, coarse_source)
    for sweep_no in range(NC - 1):
        correction = relax(
            correction,
            coarse_source,
            coarse_weight,
            2.0,
            coarse_noise,
            coarse_inverse,
            link_cols,
            "coarse",
        )
    return correction


def body(right_side, pixel_weight, noise_diag, noise_corr, neighbours):
    link_cols = lax.dynamic_slice_in_dim(neighbours, lax.axis_index("tile"), 1, 2)[:, :, 0]
    cross_noise = noise_corr * jnp.sqrt(noise_diag[0] * noise_diag[1])
    noise_terms = jnp.stack([noise_diag[0], noise_diag[1], cross_noise])
    inverse = inverse_blocks((MASS + 4.0) * pixel_weight * pixel_weight, noise_terms)
    iterate = OMEGA * apply_block(inverse, right_side)
    iterate = relax(iterate, right_side, pixel_weight, 1.0, noise_terms, inverse, link_cols, "fine")
    misfit = right_side - operate(iterate, pixel_weight, 1.0, noise_terms, link_cols, "fine")
    coarse_source = coarsen_sum(misfit)
    coarse_weight = 0.25 * coarsen_sum(pixel_weight)
    coarse_noise = coarsen_sum(noise_terms)
    correction = coarse_solve(coarse_source, coarse_weight, coarse_noise, link_cols)
    iterate = iterate + prolong(correction)
    for sweep_no in range(NU):
        iterate = relax(
            iterate, right_side, pixel_weight, 1.0, noise_terms, inverse, link_cols, "fine"
        )
    final_misfit = right_side - operate(iterate, pixel_weight, 1.0, noise_terms, link_cols, "fine")
    return (iterate, final_misfit)


def solution(mesh):
    placed = (
        P(None, ("tile", "sub"), None),
        P(("tile", "sub"), None),
        P(None, ("tile", "sub"), None),
        P(("tile", "sub"), None),
        P(),
    )
    return jax.shard_map(
        body,
        mesh=mesh,
        in_specs=placed,
        out_specs=(P(None, ("tile", "sub"), None), P(None, ("tile", "sub"), None)),
        check_vma=False,
    )
```

profile of v0, /device:TPU:2, one launch (start us, length us, event | category | flops | bytes accessed | tf_op | source)
XLA Modules:
  0.0 1307.8 jit_solution(11690635591361222974)
XLA Ops:
  15.5 3.1 psum.49
  20.0 3.7 collective-permute-start
  28.3 96.1 %all-gather.6.cloned.1.call-done = f32[128,4,2,256]{3,1,2,0:T(4,128)} async-done(((f32[1,4,2,256]{3,1,2,0:T(4,128)}), f32[128,4,2,256]{3,1,2,0:T(4,128)}) %all-gather.6.cloned.1.call-update) | async-done | bytes 1048592 | tf_op jit(solution)/shard_map/all_gather | solution.py:54
  124.4 2.8 copy.1535
  127.1 1.8 gather_fusion
  130.8 2.0 fusion.2
  134.6 3.1 psum.50
  137.8 9.8 stack.205
  147.6 18.0 %stack.204 = f32[2,64,2,128,2]{4,3,2,1,0:T(8,128)} reshape(f32[2,128,256]{2,1,0:T(8,128)S(1)} %copy-done.1) | data formatting | bytes 524288 | tf_op jit(solution)/shard_map/stack | solution.py:136
  165.6 9.7 reshape.563
  175.3 4.5 reduce_sum.27
  180.5 12.0 maximum_reduce_fusion
  192.5 2.1 collective-permute-start.2
  197.7 41.9 %all-gather.8.cloned.1.call-done = f32[128,4,2,256]{3,1,2,0:T(4,128)} async-done(((f32[1,4,2,256]{3,1,2,0:T(4,128)}), f32[128,4,2,256]{3,1,2,0:T(4,128)}) %all-gather.8.cloned.1.call-update) | async-done | bytes 1048592 | tf_op jit(solution)/shard_map/all_gather | solution.py:54
  244.0 18.1 %reshape.564 = f32[2,64,2,128,2]{4,3,2,1,0:T(8,128)} reshape(f32[2,128,256]{2,1,0:T(8,128)S(1)} %maximum_subtract_fusion.1) | data formatting | bytes 524288 | tf_op jit(solution)/shard_map/reshape | solution.py:45
  262.1 8.0 reduce_sum.29
  273.4 3.4 psum.51
  276.9 341.1 %all_gather.23 = f32[128,4,2,128]{3,1,2,0:T(4,128)S(1)} all-gather(f32[1,4,2,128]{3,1,2,0:T(4,128)S(1)} %copy.1565), channel_id=1, replica_groups=mesh['tile'=128,'sub'=2] {'tile'}, dimensions={0}, use_global_device_ids=true | all-gather | bytes 528384 | tf_op jit(solution)/shard_map/all_gather | solution.py:56
  621.1 3.0 collective-permute-start.6
  624.6 2.5 psum.52
  627.1 347.0 %all_gather.24 = f32[128,4,2,128]{3,1,2,0:T(4,128)S(1)} all-gather(f32[1,4,2,128]{3,1,2,0:T(4,128)S(1)} %copy.1573), channel_id=1, replica_groups=mesh['tile'=128,'sub'=2] {'tile'}, dimensions={0}, use_global_device_ids=true | all-gather | bytes 528384 | tf_op jit(solution)/shard_map/all_gather | solution.py:56
  976.6 3.1 psum.53
  979.8 2.1 collective-permute-start.8
  984.8 89.8 %all-gather.10.cloned.1.call-done = f32[128,4,2,256]{3,1,2,0:T(4,128)} async-done(((f32[1,4,2,256]{3,1,2,0:T(4,128)}), f32[128,4,2,256]{3,1,2,0:T(4,128)}) %all-gather.10.cloned.1.call-update) | async-done | bytes 1048592 | tf_op jit(solution)/shard_map/all_gather | solution.py:54
  1074.6 1.8 copy.1587
  1079.9 3.1 psum.54
  1083.1 2.1 collective-permute-start.10
  1088.3 96.6 %all-gather.12.cloned.1.call-done = f32[128,4,2,256]{3,1,2,0:T(4,128)} async-done(((f32[1,4,2,256]{3,1,2,0:T(4,128)}), f32[128,4,2,256]{3,1,2,0:T(4,128)}) %all-gather.12.cloned.1.call-update) | async-done | bytes 1048592 | tf_op jit(solution)/shard_map/all_gather | solution.py:54
  1190.6 3.1 psum.55
  1195.0 3.0 collective-permute-start.12
  1199.2 96.3 %all-gather.14.cloned.1.call-done = f32[128,4,2,256]{3,1,2,0:T(4,128)} async-done(((f32[1,4,2,256]{3,1,2,0:T(4,128)}), f32[128,4,2,256]{3,1,2,0:T(4,128)}) %all-gather.14.cloned.1.call-update) | async-done | bytes 1048592 | tf_op jit(solution)/shard_map/all_gather | solution.py:54
  1295.5 1.8 copy.1627
  (276 shorter events, 56.1 us)
Async XLA Ops:
  7.2 126.2 %copy-start = (f32[128,256]{1,0:T(8,128)S(1)}, f32[128,256]{1,0:T(8,128)}, u32[]{:S(2)}) copy-start(f32[128,256]{1,0:T(8,128)} %param.6) | copy-start | bytes 393220
  7.2 140.4 %copy-start.1 = (f32[2,128,256]{2,1,0:T(8,128)S(1)}, f32[2,128,256]{2,1,0:T(8,128)}, u32[]{:S(2)}) copy-start(f32[2,128,256]{2,1,0:T(8,128)} %param.7) | copy-start | bytes 786436
  7.2 117.2 %all-gather.6.cloned.1.call-start = ((), (), s32[]{:S(2)}) async-start(), calls=%async_computation | async-start | bytes 1056768 | tf_op jit(solution)/shard_map/all_gather | solution.py:54
  18.6 220.9 %all-gather.8.cloned.1.call-start = ((), (), s32[]{:S(2)}) async-start(), calls=%async_computation.1 | async-start | bytes 1056768 | tf_op jit(solution)/shard_map/all_gather | solution.py:54
  18.7 111.0 %collective-permute-start.1 = (f32[2,1,256]{1,0,2:T(2,128)}, f32[2,1,256]{1,0,2:T(2,128)}, u32[]{:S(2)}, u32[]{:S(2)}) collective-permute-start(f32[2,1,256]{1,0,2:T(2,128)} %get-tuple-element.129), channel_id=1, source_target_pairs={{1,0},{3,2},{5,4},{7,6},{9,8},{11,10},{13,12},{15,14},{17,16},{19,... | collective-permute-start | bytes 6152 | tf_op jit(solution)/shard_map/ppermute | solution.py:22
  20.0 109.3 %collective-permute-start = (f32[2,1,256]{2,0,1:T(2,128)S(1)}, f32[2,1,256]{2,0,1:T(2,128)S(1)}, u32[]{:S(2)}, u32[]{:S(2)}) collective-permute-start(f32[2,1,256]{2,0,1:T(2,128)S(1)} %copy.1640), channel_id=1, source_target_pairs={{0,1},{2,3},{4,5},{6,7},{8,9},{10,11},{12,13},{14,15},{16,17},{18,... | collective-permute-start | bytes 6152 | tf_op jit(solution)/shard_map/ppermute | solution.py:19
  137.7 936.9 %all-gather.10.cloned.1.call-start = ((), (), s32[]{:S(2)}) async-start(), calls=%async_computation.2 | async-start | bytes 1056768 | tf_op jit(solution)/shard_map/all_gather | solution.py:54
  179.9 64.0 %copy-start.2 = (f32[2,128,256]{2,1,0:T(8,128)S(1)}, f32[2,128,256]{2,1,0:T(8,128)}, u32[]{:S(2)}) copy-start(f32[2,128,256]{2,1,0:T(8,128)} %param.5) | copy-start | bytes 786436
  192.5 50.0 %collective-permute-start.2 = (f32[2,1,256]{2,1,0:T(1,128)S(1)}, f32[2,1,256]{2,1,0:T(1,128)S(1)}, u32[]{:S(2)}, u32[]{:S(2)}) collective-permute-start(f32[2,1,256]{2,1,0:T(1,128)S(1)} %get-tuple-element.122), channel_id=1, source_target_pairs={{0,1},{2,3},{4,5},{6,7},{8,9},{10,11},{12,13},{14,15},{16,17},{18,... | collective-permute-start | bytes 6152 | tf_op jit(solution)/shard_map/ppermute | solution.py:19
  194.6 47.9 %collective-permute-start.3 = (f32[2,1,256]{2,1,0:T(1,128)S(1)}, f32[2,1,256]{2,1,0:T(1,128)S(1)}, u32[]{:S(2)}, u32[]{:S(2)}) collective-permute-start(f32[2,1,256]{2,1,0:T(1,128)S(1)} %get-tuple-element.119), channel_id=1, source_target_pairs={{1,0},{3,2},{5,4},{7,6},{9,8},{11,10},{13,12},{15,14},{17,16},{19,... | collective-permute-start | bytes 6152 | tf_op jit(solution)/shard_map/ppermute | solution.py:22
  244.0 26.2 %copy-start.5 = (f32[64,128]{1,0:T(8,128)S(1)}, f32[64,128]{1,0:T(8,128)}, u32[]{:S(2)}) copy-start(f32[64,128]{1,0:T(8,128)} %get-tuple-element.155) | copy-start | bytes 98308
  244.0 375.6 %copy-start.4 = (f32[64,128]{1,0:T(8,128)S(1)}, f32[64,128]{1,0:T(8,128)}, u32[]{:S(2)}) copy-start(f32[64,128]{1,0:T(8,128)} %get-tuple-element.156) | copy-start | bytes 98308
  270.3 349.0 %collective-permute-start.4 = (f32[2,1,128]{2,0,1:T(2,128)S(1)}, f32[2,1,128]{2,0,1:T(2,128)S(1)}, u32[]{:S(2)}, u32[]{:S(2)}) collective-permute-start(f32[2,1,128]{2,0,1:T(2,128)S(1)} %bitcast.453), channel_id=1, source_target_pairs={{0,1},{2,3},{4,5},{6,7},{8,9},{10,11},{12,13},{14,15},{16,17},{18,... | collective-permute-start | bytes 3080 | tf_op jit(solution)/shard_map/ppermute | solution.py:19
  271.7 347.7 %collective-permute-start.5 = (f32[2,1,128]{2,0,1:T(2,128)S(1)}, f32[2,1,128]{2,0,1:T(2,128)S(1)}, u32[]{:S(2)}, u32[]{:S(2)}) collective-permute-start(f32[2,1,128]{2,0,1:T(2,128)S(1)} %bitcast.449), channel_id=1, source_target_pairs={{1,0},{3,2},{5,4},{7,6},{9,8},{11,10},{13,12},{15,14},{17,16},{19,... | collective-permute-start | bytes 3080 | tf_op jit(solution)/shard_map/ppermute | solution.py:22
  619.8 355.7 %collective-permute-start.7 = (f32[2,1,128]{2,0,1:T(2,128)S(1)}, f32[2,1,128]{2,0,1:T(2,128)S(1)}, u32[]{:S(2)}, u32[]{:S(2)}) collective-permute-start(f32[2,1,128]{2,0,1:T(2,128)S(1)} %bitcast.451), channel_id=1, source_target_pairs={{1,0},{3,2},{5,4},{7,6},{9,8},{11,10},{13,12},{15,14},{17,16},{19,... | collective-permute-start | bytes 3080 | tf_op jit(solution)/shard_map/ppermute | solution.py:22
  621.1 354.4 %collective-permute-start.6 = (f32[2,1,128]{2,0,1:T(2,128)S(1)}, f32[2,1,128]{2,0,1:T(2,128)S(1)}, u32[]{:S(2)}, u32[]{:S(2)}) collective-permute-start(f32[2,1,128]{2,0,1:T(2,128)S(1)} %bitcast.447), channel_id=1, source_target_pairs={{0,1},{2,3},{4,5},{6,7},{8,9},{10,11},{12,13},{14,15},{16,17},{18,... | collective-permute-start | bytes 3080 | tf_op jit(solution)/shard_map/ppermute | solution.py:19
  979.7 205.2 %all-gather.12.cloned.1.call-start = ((), (), s32[]{:S(2)}) async-start(), calls=%async_computation.3 | async-start | bytes 1056768 | tf_op jit(solution)/shard_map/all_gather | solution.py:54
  979.8 97.7 %collective-permute-start.8 = (f32[2,1,256]{2,1,0:T(1,128)S(1)}, f32[2,1,256]{2,1,0:T(1,128)S(1)}, u32[]{:S(2)}, u32[]{:S(2)}) collective-permute-start(f32[2,1,256]{2,1,0:T(1,128)S(1)} %get-tuple-element.108), channel_id=1, source_target_pairs={{0,1},{2,3},{4,5},{6,7},{8,9},{10,11},{12,13},{14,15},{16,17},{18,... | collective-permute-start | bytes 6152 | tf_op jit(solution)/shard_map/ppermute | solution.py:19
  981.9 95.7 %collective-permute-start.9 = (f32[2,1,256]{2,1,0:T(1,128)S(1)}, f32[2,1,256]{2,1,0:T(1,128)S(1)}, u32[]{:S(2)}, u32[]{:S(2)}) collective-permute-start(f32[2,1,256]{2,1,0:T(1,128)S(1)} %get-tuple-element.105), channel_id=1, source_target_pairs={{1,0},{3,2},{5,4},{7,6},{9,8},{11,10},{13,12},{15,14},{17,16},{19,... | collective-permute-start | bytes 6152 | tf_op jit(solution)/shard_map/ppermute | solution.py:22
  1083.0 212.5 %all-gather.14.cloned.1.call-start = ((), (), s32[]{:S(2)}) async-start(), calls=%async_computation.4 | async-start | bytes 1056768 | tf_op jit(solution)/shard_map/all_gather | solution.py:54
  1083.1 104.7 %collective-permute-start.10 = (f32[2,1,256]{2,1,0:T(1,128)S(1)}, f32[2,1,256]{2,1,0:T(1,128)S(1)}, u32[]{:S(2)}, u32[]{:S(2)}) collective-permute-start(f32[2,1,256]{2,1,0:T(1,128)S(1)} %get-tuple-element.94), channel_id=1, source_target_pairs={{0,1},{2,3},{4,5},{6,7},{8,9},{10,11},{12,13},{14,15},{16,17},{18,... | collective-permute-start | bytes 6152 | tf_op jit(solution)/shard_map/ppermute | solution.py:19
  1085.1 102.6 %collective-permute-start.11 = (f32[2,1,256]{2,1,0:T(1,128)S(1)}, f32[2,1,256]{2,1,0:T(1,128)S(1)}, u32[]{:S(2)}, u32[]{:S(2)}) collective-permute-start(f32[2,1,256]{2,1,0:T(1,128)S(1)} %get-tuple-element.91), channel_id=1, source_target_pairs={{1,0},{3,2},{5,4},{7,6},{9,8},{11,10},{13,12},{15,14},{17,16},{19,... | collective-permute-start | bytes 6152 | tf_op jit(solution)/shard_map/ppermute | solution.py:22
  1189.8 111.5 %copy-start.3 = (f32[2,128,256]{2,1,0:T(8,128)}, f32[2,128,256]{2,1,0:T(8,128)S(1)}, u32[]{:S(2)}) copy-start(f32[2,128,256]{2,1,0:T(8,128)S(1)} %fusion.13) | copy-start | bytes 786436
  1193.7 104.5 %collective-permute-start.13 = (f32[2,1,256]{2,1,0:T(1,128)S(1)}, f32[2,1,256]{2,1,0:T(1,128)S(1)}, u32[]{:S(2)}, u32[]{:S(2)}) collective-permute-start(f32[2,1,256]{2,1,0:T(1,128)S(1)} %get-tuple-element.77), channel_id=1, source_target_pairs={{1,0},{3,2},{5,4},{7,6},{9,8},{11,10},{13,12},{15,14},{17,16},{19,... | collective-permute-start | bytes 6152 | tf_op jit(solution)/shard_map/ppermute | solution.py:22
  1195.0 103.5 %collective-permute-start.12 = (f32[2,1,256]{2,0,1:T(2,128)S(1)}, f32[2,1,256]{2,0,1:T(2,128)S(1)}, u32[]{:S(2)}, u32[]{:S(2)}) collective-permute-start(f32[2,1,256]{2,0,1:T(2,128)S(1)} %get-tuple-element.80), channel_id=1, source_target_pairs={{0,1},{2,3},{4,5},{6,7},{8,9},{10,11},{12,13},{14,15},{16,17},{18,... | collective-permute-start | bytes 6152 | tf_op jit(solution)/shard_map/ppermute | solution.py:19
Sparse Core Ops, SparseCore 0:
  18.8 105.5 all-gather.5
  137.9 101.6 all-gather.7
  979.8 94.7 all-gather.9
  1083.1 101.6 all-gather.11
  1193.8 101.6 all-gather.13
where the time goes:
time: 1310 us
  blocking collectives  710 us (54%)
  waiting for transfers between devices  421 us (32%)
  local copies, waits for them, and re-layouts  94.2 us (7%)
  other arithmetic  41.1 us (3%)
  starting transfers between devices  26.9 us (2%)
  between operations  15.2 us (1%)
    all_gather x2, blocking collectives, across_sides(): everyone = lax.all_gather(side_rows[None], 'tile', axis=0, tiled=True)  688 us
    all_gather x5, waiting for transfers between devices, across_sides(): everyone = lax.all_gather(side_rows[None], 'tile', axis=0, tiled=True)  421 us
    another operation x2, local copies, waits for them, and re-layouts, body(): noise_terms = jnp.stack([noise_diag[0], noise_diag[1], cross_noise])  27.8 us
    reshape x2, local copies, waits for them, and re-layouts, coarsen_sum(): return values.reshape(new_shape).sum(axis=(-3, -1))  27.8 us
  transfers between devices with their start and end apart: 19, of which 5 were waited for; matrix products, arithmetic and copies ran while one was open for 7% of the time, Pallas kernels for 0%

commit v1 on v0

v1 whole, which is shorter than its diff:
```python
import functools

import jax
import jax.numpy as jnp
from jax import lax
from jax.experimental import pallas as pl
from jax.experimental.pallas import tpu as pltpu
from jax.sharding import PartitionSpec as P

MASS = 0.05
OMEGA = 0.8
KEEP = 1.0 - OMEGA
CENTRE = MASS + 4.0
TS = 256
HALF = 128
TILES = 128
CHUNK = 8
CHUNKS = TS // CHUNK
MESH = pl.DeviceIdType.MESH

LINE_OFFS = [-3, -2, -1, 1, 2, 3] + [64 + d for d in range(-3, 4)]
CORNER_OFFS = [-6, -5, -4, -3, -2, -1, 1, 2, 3, 4, 5, 6] + [64 + d for d in range(-6, 7)]


def slot_of(distance, reach):
    d = lax.rem(distance + TILES, TILES)
    far = d - (64 - reach) + 2 * reach
    near = jnp.where(d <= reach, d + reach - 1, d - (TILES - reach))
    slot = jnp.where((d <= reach) | (d >= TILES - reach), near, far)
    slot = jnp.where(d == 0, 4 * reach + 1, slot)
    return jnp.minimum(jnp.maximum(slot, 0), 4 * reach + 1)


def lanes(rows, cols):
    return lax.broadcasted_iota(jnp.int32, (rows, cols), 1)


def pair_sum(x):
    lane = lanes(CHUNK, TS)
    x = x + jnp.where(lane % 2 == 0, pltpu.roll(x, TS - 1, 1), pltpu.roll(x, 1, 1))
    row = lax.broadcasted_iota(jnp.int32, (CHUNK, TS), 0)
    return x + jnp.where(row % 2 == 0, pltpu.roll(x, CHUNK - 1, 0), pltpu.roll(x, 1, 0))


def smoother_terms(stiffness, w, n0, n1, cross, f0, f1):
    diag = (stiffness * CENTRE) * w * w
    b00, b11 = diag + n0, diag + n1
    scale = OMEGA / (b00 * b11 - cross * cross)
    k00, k11, k01 = scale * b11, scale * b00, -(scale * cross)
    v0 = w * (k00 * f0 + k01 * f1)
    v1 = w * (k01 * f0 + k11 * f1)
    ww = stiffness * w * w
    return v0, v1, ww * k00, ww * k11, ww * k01


def kernel(
    nb, rs_in, w_in, nd_in, nc_in, sol_out, mis_out,
    rs, wt, nd, nc, iw, kf, kc, sf, sc, wiw, va, vb, ca, cb,
    ec, ect, hs, hc, st1, st2, st3, st4, re1, re2, re3, re4, nb1, nb2, nb3, nb4,
    cs1, cs2, cs3, cr1, cr2, cr3, lsem, psem, prem, ssem, rsem, cssem, crsem,
):
    cst, cre = (cs1, cs2, cs3), (cr1, cr2, cr3)
    t = lax.axis_index("tile")
    c = lax.axis_index("sub")
    band = pl.multiple_of(c * HALF, HALF)

    def tile_at(offset):
        return (lax.rem(t + (offset + TILES), TILES), c)

    barrier = pltpu.get_barrier_semaphore()
    for o in CORNER_OFFS:
        pl.semaphore_signal(barrier, inc=1, device_id=tile_at(o), device_id_type=MESH)
    pl.semaphore_signal(barrier, inc=1, device_id=(t, 1 - c), device_id_type=MESH)

    rows = pl.ds(band, HALF)
    moves = [
        (rs_in.at[0], rs.at[0, rows]), (rs_in.at[1], rs.at[1, rows]), (w_in, wt.at[rows]),
        (nd_in.at[0], nd.at[0, rows]), (nd_in.at[1], nd.at[1, rows]), (nc_in, nc.at[rows]),
    ]
    local = [pltpu.make_async_copy(s, d, lsem.at[i]) for i, (s, d) in enumerate(moves)]
    for m in local:
        m.start()
    pl.semaphore_wait(barrier, len(CORNER_OFFS) + 1)
    shared = [
        pltpu.make_async_remote_copy(
            s, d, psem.at[i], prem.at[i], device_id=(t, 1 - c), device_id_type=MESH
        )
        for i, (s, d) in enumerate(moves)
    ]
    for m in shared:
        m.start()

    flip, line_slot, ghost = [], [], {}
    for k in range(4):
        n, f = nb[0, k, t], nb[2, k, t]
        flip.append(f)
        line_slot.append(slot_of(n - t, 3))
        base = 2 if k < 2 else 0
        for e in range(2):
            end = jnp.where(f == 1, 1 - e, e)
            q = base + end
            m, g = nb[0, q, n], nb[2, q, n]
            place = (k ^ 1) % 2
            ghost[k, e] = (slot_of(m - t, 6), end, jnp.where(g == 1, 1 - place, place))

    def send(x, stage, land, width):
        for o in LINE_OFFS:
            i = LINE_OFFS.index((-o + 3) % TILES - 3)
            pltpu.make_async_remote_copy(
                stage, land.at[i], ssem.at[x], rsem.at[x], device_id=tile_at(o), device_id_type=MESH
            ).start()
        if x < 3:
            lane = lanes(2, HALF)
            for k in range(4):
                pair = stage[k, 0:2, :]
                cst[x][2 * k : 2 * k + 2, :] = jnp.where(lane < 64, pair[:, :HALF], pair[:, HALF:])
            for o in CORNER_OFFS:
                i = CORNER_OFFS.index((-o + 6) % TILES - 6)
                pltpu.make_async_remote_copy(
                    cst[x], cre[x].at[i], cssem.at[x], crsem.at[x], device_id=tile_at(o), device_id_type=MESH
                ).start()
            cre[x][len(CORNER_OFFS)] = cst[x][...]
        land[len(LINE_OFFS)] = stage[...]

    def receive(x, land, width, near):
        got = land.at[pl.ds(0, len(LINE_OFFS))]
        pltpu.make_async_copy(got, got, rsem.at[x]).wait()
        for k in range(4):
            near[k * width : (k + 1) * width, :] = land[line_slot[k], k ^ 1]
        back = (HALF - 1) - lanes(8, HALF)
        for b in range(0, 4 * width, 8):
            v = near[b : b + 8, :]
            turned = jnp.concatenate(
                [
                    jnp.take_along_axis(v[:, HALF:], back, axis=1),
                    jnp.take_along_axis(v[:, :HALF], back, axis=1),
                ],
                axis=1,
            )
            side = (lax.broadcasted_iota(jnp.int32, (8, TS), 0) + b) // width
            flag = jnp.where(
                side < 2, jnp.where(side == 0, flip[0], flip[1]), jnp.where(side == 2, flip[2], flip[3])
            )
            near[b : b + 8, :] = jnp.where(flag == 1, turned, v)

    def corners(x):
        got = cre[x].at[pl.ds(0, len(CORNER_OFFS))]
        pltpu.make_async_copy(got, got, crsem.at[x]).wait()
        values = {}
        for k in range(4):
            low = 4 if k < 2 else 0
            for e in range(2):
                slot, end, place = ghost[k, e]
                block = cre[x][slot]
                pair = jnp.where(end == 1, block[low : low + 2, :], block[low + 2 : low + 4, :])
                values[k, e] = jnp.where(place == 1, pair[:, HALF - 1 :], pair[:, :1])
        return values

    def advance(near, width, stage, s, ghosts, outer, terms):
        lane = lanes(1, TS)
        out = []
        for k in range(4):
            line = [near[k * width + j : k * width + j + 1, :] for j in range(2)]
            sums = []
            for j in range(2):
                low = jnp.where(lane < s, ghosts[k, 0][j : j + 1, :], pltpu.roll(line[j], s, 1))
                high = jnp.where(lane >= TS - s, ghosts[k, 1][j : j + 1, :], pltpu.roll(line[j], TS - s, 1))
                beyond = near[k * width + outer + j : k * width + outer + j + 1, :]
                sums.append(low + high + beyond + stage[k, j : j + 1, :])
            start0, start1, k00, k11, k01 = terms(k)
            out.append(
                [
                    KEEP * line[0] + start0 + (k00 * sums[0] + k01 * sums[1]),
                    KEEP * line[1] + start1 + (k01 * sums[0] + k11 * sums[1]),
                ]
            )
        return out

    def set_halo(v, s, lines):
        for j in range(2):
            for i in range(s):
                v[j, 7 - i : 8 - i, :] = lines[0][j]
                v[j, 264 + i : 265 + i, :] = lines[1][j]
                hs[j, i : i + 1, :] = lines[2][j]
                hs[j, HALF - 1 - i : HALF - i, :] = lines[3][j]
            hc[j] = jnp.transpose(hs[j])

    def plain_lines(near, width):
        return [[near[k * width + j : k * width + j + 1, :] for j in range(2)] for k in range(4)]

    def beside(v, j, r, s):
        lane = lanes(CHUNK, TS)
        here = v[j, pl.ds(r + 8, CHUNK), :]
        row = lax.broadcasted_iota(jnp.int32, (CHUNK, TS), 0)
        above = pltpu.roll(jnp.where(row >= CHUNK - s, v[j, pl.ds(r, CHUNK), :], here), s, 0)
        below = pltpu.roll(jnp.where(row < s, v[j, pl.ds(r + 16, CHUNK), :], here), CHUNK - s, 0)
        edge = hc[j, pl.ds(r, CHUNK), :]
        edge = jnp.concatenate([edge, edge], axis=1)
        west = jnp.where(lane < s, edge, pltpu.roll(here, s, 1))
        east = jnp.where(lane >= TS - s, edge, pltpu.roll(here, TS - s, 1))
        return here, (above + below) + (west + east)

    def put_edges(r, q, u, extra=()):
        lane = lanes(CHUNK, HALF)
        out = jnp.where(lane < 64, pltpu.roll(u[:, :HALF], 3, 1), pltpu.roll(u[:, HALF:], HALF - 3, 1))
        out = jnp.where(lane < 3, q[:, :HALF], jnp.where(lane >= HALF - 3, q[:, HALF:], out))
        for i, x in enumerate(extra):
            out = jnp.where(lane == 6 + i, pltpu.roll(x[:, :HALF], 6 + i, 1), out)
            out = jnp.where(lane == HALF - 7 - i, pltpu.roll(x[:, HALF:], HALF - 6 - i, 1), out)
        ec[pl.ds(r, CHUNK), :] = out

    def fill_stage(stage, v, s, second, terms):
        ect[...] = jnp.transpose(ec[...])
        for j in range(2):
            stage[0, j : j + 1, :] = v[j, 8:9, :]
            stage[1, j : j + 1, :] = v[j, 263:264, :]
            stage[2, j : j + 1, :] = ect[3 * j : 3 * j + 1, :]
            stage[3, j : j + 1, :] = ect[127 - 3 * j : 128 - 3 * j, :]
            if second is not None:
                b = second + j
                stage[0, b : b + 1, :] = v[j, 8 + s : 9 + s, :]
                stage[1, b : b + 1, :] = v[j, 263 - s : 264 - s, :]
                stage[2, b : b + 1, :] = ect[3 * j + s : 3 * j + s + 1, :]
                stage[3, b : b + 1, :] = ect[127 - 3 * j - s : 128 - 3 * j - s, :]
        if terms is not None:
            for i in range(3):
                stage[0, 2 + i : 3 + i, :] = terms[i, 0:1, :]
                stage[1, 2 + i : 3 + i, :] = terms[i, TS - 1 : TS, :]
                stage[2, 2 + i : 3 + i, :] = ect[6 + i : 7 + i, :]
                stage[3, 2 + i : 3 + i, :] = ect[121 - i : 122 - i, :]
            stage[:, 7:8, :] = jnp.zeros((4, 1, TS), jnp.float32)

    def over_chunks(step, first=0, count=CHUNKS):
        def body(i, carry):
            step(pl.multiple_of(first + i * CHUNK, CHUNK))
            return carry
        lax.fori_loop(0, count, body, 0)

    def sweep(src, start, terms, s, r):
        q, nq = beside(src, 0, r, s)
        u, nu = beside(src, 1, r, s)
        here = pl.ds(r, CHUNK)
        k00, k11, k01 = terms[0, here, :], terms[1, here, :], terms[2, here, :]
        q = KEEP * q + start[0, here, :] + (k00 * nq + k01 * nu)
        u = KEEP * u + start[1, here, :] + (k01 * nq + k11 * nu)
        return q, u

    def residual(src, r):
        here = pl.ds(r, CHUNK)
        q, nq = beside(src, 0, r, 1)
        u, nu = beside(src, 1, r, 1)
        w, cross, inv = wt[here, :], nc[here, :], iw[here, :]
        q0, u0 = q * inv, u * inv
        mq = rs[0, here, :] - (w * (CENTRE * q - nq) + nd[0, here, :] * q0 + cross * u0)
        mu = rs[1, here, :] - (w * (CENTRE * u - nu) + cross * q0 + nd[1, here, :] * u0)
        return mq, mu, q0, u0

    hs[...] = jnp.zeros_like(hs)
    for m in local + shared:
        m.wait()

    def start_fine(r):
        here = pl.ds(r, CHUNK)
        n0, n1, w = nd[0, here, :], nd[1, here, :], wt[here, :]
        cross = nc[here, :] * jnp.sqrt(n0 * n1)
        nc[here, :] = cross
        iw[here, :] = 1.0 / w
        q, u, k00, k11, k01 = smoother_terms(1.0, w, n0, n1, cross, rs[0, here, :], rs[1, here, :])
        kf[0, here, :], kf[1, here, :], kf[2, here, :] = k00, k11, k01
        sf[0, here, :], sf[1, here, :] = q, u
        va[0, pl.ds(r + 8, CHUNK), :], va[1, pl.ds(r + 8, CHUNK), :] = q, u
        put_edges(r, q, u, (k00, k11, k01))

    over_chunks(start_fine)
    fill_stage(st1, va, 1, 5, kf)
    send(0, st1, re1, 8)
    receive(0, re1, 8, nb1)
    set_halo(va, 1, plain_lines(nb1, 8))

    def first_sweep(r):
        q, u = sweep(va, sf, kf, 1, r)
        vb[0, pl.ds(r + 8, CHUNK), :], vb[1, pl.ds(r + 8, CHUNK), :] = q, u

    over_chunks(first_sweep)

    def terms_of(near):
        def terms(k):
            return [near[k * 8 + j : k * 8 + j + 1, :] for j in (0, 1, 2, 3, 4)]
        return terms

    set_halo(vb, 1, advance(nb1, 8, st1, 1, corners(0), 5, terms_of(nb1)))

    def start_coarse(r):
        here = pl.ds(r, CHUNK)
        mq, mu, _, _ = residual(vb, r)
        w = wt[here, :]
        cw = 0.25 * pair_sum(w)
        wiw[here, :] = w / cw
        q, u, k00, k11, k01 = smoother_terms(
            2.0, cw, pair_sum(nd[0, here, :]), pair_sum(nd[1, here, :]), pair_sum(nc[here, :]),
            pair_sum(mq), pair_sum(mu),
        )
        kc[0, here, :], kc[1, here, :], kc[2, here, :] = k00, k11, k01
        sc[0, here, :], sc[1, here, :] = q, u
        ca[0, pl.ds(r + 8, CHUNK), :], ca[1, pl.ds(r + 8, CHUNK), :] = q, u
        put_edges(r, q, u, (k00, k11, k01))

    over_chunks(start_coarse)
    fill_stage(st2, ca, 2, 5, kc)
    send(1, st2, re2, 8)
    receive(1, re2, 8, nb2)
    set_halo(ca, 2, plain_lines(nb2, 8))

    def coarse_sweep(r):
        q, u = sweep(ca, sc, kc, 2, r)
        cb[0, pl.ds(r + 8, CHUNK), :], cb[1, pl.ds(r + 8, CHUNK), :] = q, u

    over_chunks(coarse_sweep)
    set_halo(cb, 2, advance(nb2, 8, st2, 2, corners(1), 5, terms_of(nb2)))

    def correct(r):
        q, u = sweep(cb, sc, kc, 2, r)
        up = wiw[pl.ds(r, CHUNK), :]
        here = pl.ds(r + 8, CHUNK)
        q, u = vb[0, here, :] + up * q, vb[1, here, :] + up * u
        va[0, here, :], va[1, here, :] = q, u
        put_edges(r, q, u)

    over_chunks(correct)
    fill_stage(st3, va, 1, 2, None)
    send(2, st3, re3, 4)
    receive(2, re3, 4, nb3)
    set_halo(va, 1, plain_lines(nb3, 4))
    over_chunks(first_sweep)
    set_halo(vb, 1, advance(nb3, 4, st3, 1, corners(2), 2, terms_of(nb1)))

    def last_sweep(r):
        q, u = sweep(vb, sf, kf, 1, r)
        va[0, pl.ds(r + 8, CHUNK), :], va[1, pl.ds(r + 8, CHUNK), :] = q, u
        put_edges(r, q, u)

    over_chunks(last_sweep)
    fill_stage(st4, va, 1, None, None)
    send(3, st4, re4, 2)
    receive(3, re4, 2, nb4)
    set_halo(va, 1, plain_lines(nb4, 2))

    def finish(i, carry):
        r = pl.multiple_of(band + i * CHUNK, CHUNK)
        mq, mu, q, u = residual(va, r)
        here = pl.ds(pl.multiple_of(i * CHUNK, CHUNK), CHUNK)
        sol_out[0, here, :], sol_out[1, here, :] = q, u
        mis_out[0, here, :], mis_out[1, here, :] = mq, mu
        return carry

    lax.fori_loop(0, HALF // CHUNK, finish, 0)

    for x, land in enumerate((re1, re2, re3, re4)):
        sent = land.at[pl.ds(0, len(LINE_OFFS))]
        pltpu.make_async_copy(sent, sent, ssem.at[x]).wait()
        if x < 3:
            sent = cre[x].at[pl.ds(0, len(CORNER_OFFS))]
            pltpu.make_async_copy(sent, sent, cssem.at[x]).wait()


def body(right_side, pixel_weight, noise_diag, noise_corr, neighbours):
    f32 = jnp.float32
    vm = pltpu.VMEM
    plane, pair, triple, padded = (TS, TS), (2, TS, TS), (3, TS, TS), (2, TS + 16, TS)
    hbm = pl.BlockSpec(memory_space=pl.ANY)
    widths = (8, 8, 4, 2)
    dma = pltpu.SemaphoreType.DMA
    return pl.pallas_call(
        kernel,
        out_shape=[jax.ShapeDtypeStruct((2, HALF, TS), f32)] * 2,
        in_specs=[pl.BlockSpec(memory_space=pltpu.SMEM), hbm, hbm, hbm, hbm],
        out_specs=[pl.BlockSpec(memory_space=pltpu.VMEM)] * 2,
        scratch_shapes=[
            vm(pair, f32), vm(plane, f32), vm(pair, f32), vm(plane, f32), vm(plane, f32),
            vm(triple, f32), vm(triple, f32), vm(pair, f32), vm(pair, f32), vm(plane, f32),
            vm(padded, f32), vm(padded, f32), vm(padded, f32), vm(padded, f32),
            vm((TS, HALF), f32), vm((HALF, TS), f32), vm((2, HALF, TS), f32), vm((2, TS, HALF), f32),
        ]
        + [vm((4, n, TS), f32) for n in widths]
        + [vm((14, 4, n, TS), f32) for n in widths]
        + [vm((4 * n, TS), f32) for n in widths]
        + [
            *[vm((8, HALF), f32)] * 3, *[vm((26, 8, HALF), f32)] * 3,
            dma((6,)), dma((6,)), dma((6,)), dma((4,)), dma((4,)), dma((3,)), dma((3,)),
        ],
        compiler_params=pltpu.CompilerParams(
            collective_id=0, has_side_effects=True, vmem_limit_bytes=48 * 2**20
        ),
    )(neighbours, right_side, pixel_weight, noise_diag, noise_corr)


def solution(mesh):
    placed = (
        P(None, ("tile", "sub"), None),
        P(("tile", "sub"), None),
        P(None, ("tile", "sub"), None),
        P(("tile", "sub"), None),
        P(),
    )
    return jax.shard_map(
        body,
        mesh=mesh,
        in_specs=placed,
        out_specs=(P(None, ("tile", "sub"), None), P(None, ("tile", "sub"), None)),
        check_vma=False,
    )
```

time: 1310 us -> 85 us (0.06)
  blocking collectives: 710 us -> 0 us
  waiting for transfers between devices: 421 us -> 0 us
  local copies, waits for them, and re-layouts: 94.2 us -> 5.8 us
  Pallas kernels: 0 us -> 78.3 us
  other arithmetic: 41.1 us -> 0 us
  starting transfers between devices: 26.9 us -> 0 us
  between operations: 15.2 us -> 0.65 us
    all_gather x2 -> x0, blocking collectives: 688 us -> none  [across_sides(): everyone = lax.all_gather(side_rows[None], 'tile', axis=0, tiled=True)]
    all_gather x5 -> x0, waiting for transfers between devices: 421 us -> none  [across_sides(): everyone = lax.all_gather(side_rows[None], 'tile', axis=0, tiled=True)]
    pallas_call x0 -> x1, Pallas kernels: none -> 78.3 us  [body(): pl.pallas_call(kernel, out_shape=[jax.ShapeDtypeStruct((2, HALF, TS), f32...]
    another operation x22 -> x0, local copies, waits for them, and re-layouts: 29.4 us -> none  [the longest x2 27.8 us: body(): noise_terms = jnp.stack([noise_diag[0], noise_diag[1], cross_noise])]
    reshape x4 -> x0, local copies, waits for them, and re-layouts: 28 us -> none  [the longest x2 27.8 us: coarsen_sum(): return values.reshape(new_shape).sum(axis=(-3, -1))]
    ppermute x14 -> x0, starting transfers between devices: 26.7 us -> none  [the longest x7 17.3 us: with_halo(): lax.ppermute(lax.slice_in_dim(block, block.shape[dim] - width, None, axis...]
    reduce_sum x3 -> x0, other arithmetic: 24.5 us -> none  [coarsen_sum(): return values.reshape(new_shape).sum(axis=(-3, -1))]
    psum x7 -> x0, blocking collectives: 21.3 us -> none  [band_sum(): side_rows = lax.psum(partial_sides, 'sub')]
  transfers between devices with their start and end apart: 19 -> 0, of which waited for: 5 -> 0; matrix products, arithmetic and copies ran while one was open for 7% -> 0% of each run, Pallas kernels for 0% -> 0%
where the time goes in v1:
time: 85 us; the launch traced here: 84.8 us
  Pallas kernels  78.3 us (92%)
  local copies, waits for them, and re-layouts  5.8 us (7%)
    pallas_call x1, Pallas kernels, body(): pl.pallas_call(kernel, out_shape=[jax.ShapeDtypeStruct((2, HALF, TS), f32...  78.3 us
    unnamed x12, local copies, waits for them, and re-layouts  5.8 us

profile of v1, /device:TPU:2, one launch (start us, length us, event | category | flops | bytes accessed | tf_op | source)
XLA Modules:
  0.0 84.8 jit_solution(11602481993805419109)
XLA Ops:
  0.6 0.0 copy-start
  0.6 0.9 %copy-done = f32[2,128,256]{2,1,0:T(8,128)S(1)} copy-done((f32[2,128,256]{2,1,0:T(8,128)S(1)}, f32[2,128,256]{2,1,0:T(8,128)}, u32[]{:S(2)}) %copy-start) | copy-done | bytes 262168
  1.6 0.0 copy-start.1
  1.6 0.9 %copy-done.1 = f32[2,128,256]{2,1,0:T(8,128)S(1)} copy-done((f32[2,128,256]{2,1,0:T(8,128)S(1)}, f32[2,128,256]{2,1,0:T(8,128)}, u32[]{:S(2)}) %copy-start.1) | copy-done | bytes 262168
  2.5 0.0 copy-start.2
  2.5 0.9 %copy-done.2 = f32[128,256]{1,0:T(8,128)S(1)} copy-done((f32[128,256]{1,0:T(8,128)S(1)}, f32[128,256]{1,0:T(8,128)}, u32[]{:S(2)}) %copy-start.2) | copy-done | bytes 131096
  3.4 0.0 copy-start.3
  3.4 0.9 %copy-done.3 = f32[128,256]{1,0:T(8,128)S(1)} copy-done((f32[128,256]{1,0:T(8,128)S(1)}, f32[128,256]{1,0:T(8,128)}, u32[]{:S(2)}) %copy-start.3) | copy-done | bytes 131096
  4.3 0.0 copy-start.4
  4.3 0.7 copy-done.4
  5.0 78.3 %shard_map.68 = (f32[2,128,256]{2,1,0:T(8,128)S(1)}, f32[2,128,256]{2,1,0:T(8,128)S(1)}) custom-call(s32[3,4,128]{2,1,0:T(4,128)S(1)} %copy-done.4, f32[2,128,256]{2,1,0:T(8,128)S(1)} %copy-done, f32[128,256]{1,0:T(8,128)S(1)} %copy-done.2, f32[2,128,256]{2,1,0:T(8,128)S(1)} %copy-done.1, f32[128,256]{1,0:T(8,128)S(1)} %copy-done.3), custom_call_target="tpu_custom_call" | custom-call | tf_op jit(solution)/shard_map/pallas_call | solution.py:373
  83.4 0.7 copy.9
  84.1 0.7 copy.10
Async XLA Ops:
  0.6 1.0 %copy-start = (f32[2,128,256]{2,1,0:T(8,128)S(1)}, f32[2,128,256]{2,1,0:T(8,128)}, u32[]{:S(2)}) copy-start(f32[2,128,256]{2,1,0:T(8,128)} %rs_in.1) | copy-start | bytes 786436
  1.6 0.9 %copy-start.1 = (f32[2,128,256]{2,1,0:T(8,128)S(1)}, f32[2,128,256]{2,1,0:T(8,128)}, u32[]{:S(2)}) copy-start(f32[2,128,256]{2,1,0:T(8,128)} %nd_in.1) | copy-start | bytes 786436
  2.5 0.9 %copy-start.2 = (f32[128,256]{1,0:T(8,128)S(1)}, f32[128,256]{1,0:T(8,128)}, u32[]{:S(2)}) copy-start(f32[128,256]{1,0:T(8,128)} %w_in.1) | copy-start | bytes 393220
  3.4 0.9 %copy-start.3 = (f32[128,256]{1,0:T(8,128)S(1)}, f32[128,256]{1,0:T(8,128)}, u32[]{:S(2)}) copy-start(f32[128,256]{1,0:T(8,128)} %nc_in.1) | copy-start | bytes 393220
  4.3 0.7 copy-start.4

commit v2 on v1

--- a/solution.py
+++ b/solution.py
@@ -16,6 +16,7 @@
 TILES = 128
 CHUNK = 8
 CHUNKS = TS // CHUNK
+BATCH = 4
 MESH = pl.DeviceIdType.MESH
 
 LINE_OFFS = [-3, -2, -1, 1, 2, 3] + [64 + d for d in range(-3, 4)]
@@ -232,9 +233,10 @@
 
     def over_chunks(step, first=0, count=CHUNKS):
         def body(i, carry):
-            step(pl.multiple_of(first + i * CHUNK, CHUNK))
+            for b in range(BATCH):
+                step(pl.multiple_of(first + (i * BATCH + b) * CHUNK, CHUNK))
             return carry
-        lax.fori_loop(0, count, body, 0)
+        lax.fori_loop(0, count // BATCH, body, 0)
 
     def sweep(src, start, terms, s, r):
         q, nq = beside(src, 0, r, s)
@@ -345,15 +347,14 @@
     receive(3, re4, 2, nb4)
     set_halo(va, 1, plain_lines(nb4, 2))
 
-    def finish(i, carry):
-        r = pl.multiple_of(band + i * CHUNK, CHUNK)
+    def finish(i):
+        r = pl.multiple_of(band + i, CHUNK)
         mq, mu, q, u = residual(va, r)
-        here = pl.ds(pl.multiple_of(i * CHUNK, CHUNK), CHUNK)
+        here = pl.ds(i, CHUNK)
         sol_out[0, here, :], sol_out[1, here, :] = q, u
         mis_out[0, here, :], mis_out[1, here, :] = mq, mu
-        return carry
-
-    lax.fori_loop(0, HALF // CHUNK, finish, 0)
+
+    over_chunks(finish, 0, HALF // CHUNK)
 
     for x, land in enumerate((re1, re2, re3, re4)):
         sent = land.at[pl.ds(0, len(LINE_OFFS))]

time: 85 us -> 64.5 us (0.76)
  Pallas kernels: 78.3 us -> 57.8 us
    pallas_call x1, Pallas kernels: 78.3 us -> 57.8 us  [body(): pl.pallas_call(kernel, out_shape=[jax.ShapeDtypeStruct((2, HALF, TS), f32...]
where the time goes in v2:
time: 64.5 us; the launch traced here: 64.3 us
  Pallas kernels  57.8 us (90%)
  local copies, waits for them, and re-layouts  5.8 us (9%)
  between operations  0.65 us (1%)
    pallas_call x1, Pallas kernels, body(): pl.pallas_call(kernel, out_shape=[jax.ShapeDtypeStruct((2, HALF, TS), f32...  57.8 us
    unnamed x12, local copies, waits for them, and re-layouts  5.8 us

profile of v2, /device:TPU:2, one launch (start us, length us, event | category | flops | bytes accessed | tf_op | source)
XLA Modules:
  0.0 64.3 jit_solution(14053986988482195525)
XLA Ops:
  0.6 0.0 copy-start
  0.6 0.9 %copy-done = f32[2,128,256]{2,1,0:T(8,128)S(1)} copy-done((f32[2,128,256]{2,1,0:T(8,128)S(1)}, f32[2,128,256]{2,1,0:T(8,128)}, u32[]{:S(2)}) %copy-start) | copy-done | bytes 262168
  1.6 0.0 copy-start.1
  1.6 0.9 %copy-done.1 = f32[2,128,256]{2,1,0:T(8,128)S(1)} copy-done((f32[2,128,256]{2,1,0:T(8,128)S(1)}, f32[2,128,256]{2,1,0:T(8,128)}, u32[]{:S(2)}) %copy-start.1) | copy-done | bytes 262168
  2.5 0.0 copy-start.2
  2.5 0.9 %copy-done.2 = f32[128,256]{1,0:T(8,128)S(1)} copy-done((f32[128,256]{1,0:T(8,128)S(1)}, f32[128,256]{1,0:T(8,128)}, u32[]{:S(2)}) %copy-start.2) | copy-done | bytes 131096
  3.4 0.0 copy-start.3
  3.4 0.9 %copy-done.3 = f32[128,256]{1,0:T(8,128)S(1)} copy-done((f32[128,256]{1,0:T(8,128)S(1)}, f32[128,256]{1,0:T(8,128)}, u32[]{:S(2)}) %copy-start.3) | copy-done | bytes 131096
  4.3 0.0 copy-start.4
  4.3 0.7 %copy-done.4 = s32[3,4,128]{2,1,0:T(4,128)S(1)} copy-done((s32[3,4,128]{2,1,0:T(4,128)S(1)}, s32[3,4,128]{2,1,0:T(4,128)}, u32[]{:S(2)}) %copy-start.4) | copy-done | bytes 6168
  5.0 57.8 %shard_map.68 = (f32[2,128,256]{2,1,0:T(8,128)S(1)}, f32[2,128,256]{2,1,0:T(8,128)S(1)}) custom-call(s32[3,4,128]{2,1,0:T(4,128)S(1)} %copy-done.4, f32[2,128,256]{2,1,0:T(8,128)S(1)} %copy-done, f32[128,256]{1,0:T(8,128)S(1)} %copy-done.2, f32[2,128,256]{2,1,0:T(8,128)S(1)} %copy-done.1, f32[128,256]{1,0:T(8,128)S(1)} %copy-done.3), custom_call_target="tpu_custom_call" | custom-call | tf_op jit(solution)/shard_map/pallas_call | solution.py:374
  62.9 0.7 %copy.9 = f32[2,128,256]{2,1,0:T(8,128)} copy(f32[2,128,256]{2,1,0:T(8,128)S(1)} %get-tuple-element.4) | data formatting | bytes 524288
  63.6 0.7 %copy.10 = f32[2,128,256]{2,1,0:T(8,128)} copy(f32[2,128,256]{2,1,0:T(8,128)S(1)} %get-tuple-element.5) | data formatting | bytes 524288
Async XLA Ops:
  0.6 1.0 %copy-start = (f32[2,128,256]{2,1,0:T(8,128)S(1)}, f32[2,128,256]{2,1,0:T(8,128)}, u32[]{:S(2)}) copy-start(f32[2,128,256]{2,1,0:T(8,128)} %rs_in.1) | copy-start | bytes 786436
  1.6 0.9 %copy-start.1 = (f32[2,128,256]{2,1,0:T(8,128)S(1)}, f32[2,128,256]{2,1,0:T(8,128)}, u32[]{:S(2)}) copy-start(f32[2,128,256]{2,1,0:T(8,128)} %nd_in.1) | copy-start | bytes 786436
  2.5 0.9 %copy-start.2 = (f32[128,256]{1,0:T(8,128)S(1)}, f32[128,256]{1,0:T(8,128)}, u32[]{:S(2)}) copy-start(f32[128,256]{1,0:T(8,128)} %w_in.1) | copy-start | bytes 393220
  3.4 0.9 %copy-start.3 = (f32[128,256]{1,0:T(8,128)S(1)}, f32[128,256]{1,0:T(8,128)}, u32[]{:S(2)}) copy-start(f32[128,256]{1,0:T(8,128)} %nc_in.1) | copy-start | bytes 393220
  4.3 0.7 %copy-start.4 = (s32[3,4,128]{2,1,0:T(4,128)S(1)}, s32[3,4,128]{2,1,0:T(4,128)}, u32[]{:S(2)}) copy-start(s32[3,4,128]{2,1,0:T(4,128)} %nb.1) | copy-start | bytes 18436

commit v3 on v2

--- a/solution.py
+++ b/solution.py
@@ -58,7 +58,8 @@
     nb, rs_in, w_in, nd_in, nc_in, sol_out, mis_out,
     rs, wt, nd, nc, iw, kf, kc, sf, sc, wiw, va, vb, ca, cb,
     ec, ect, hs, hc, st1, st2, st3, st4, re1, re2, re3, re4, nb1, nb2, nb3, nb4,
-    cs1, cs2, cs3, cr1, cr2, cr3, lsem, psem, prem, ssem, rsem, cssem, crsem,
+    cs1, cs2, cs3, cr1, cr2, cr3, mo1, mo2, mo3, mr1, mr2, mr3, nm1, nm2, nm3,
+    lsem, psem, prem, ssem, rsem, cssem, crsem, msem, mrsem,
 ):
     cst, cre = (cs1, cs2, cs3), (cr1, cr2, cr3)
     t = lax.axis_index("tile")
@@ -104,28 +105,34 @@
             place = (k ^ 1) % 2
             ghost[k, e] = (slot_of(m - t, 6), end, jnp.where(g == 1, 1 - place, place))
 
-    def send(x, stage, land, width):
+    def spread(stage, land, gone, come):
         for o in LINE_OFFS:
             i = LINE_OFFS.index((-o + 3) % TILES - 3)
             pltpu.make_async_remote_copy(
-                stage, land.at[i], ssem.at[x], rsem.at[x], device_id=tile_at(o), device_id_type=MESH
+                stage, land.at[i], gone, come, device_id=tile_at(o), device_id_type=MESH
             ).start()
-        if x < 3:
-            lane = lanes(2, HALF)
-            for k in range(4):
-                pair = stage[k, 0:2, :]
-                cst[x][2 * k : 2 * k + 2, :] = jnp.where(lane < 64, pair[:, :HALF], pair[:, HALF:])
-            for o in CORNER_OFFS:
-                i = CORNER_OFFS.index((-o + 6) % TILES - 6)
-                pltpu.make_async_remote_copy(
-                    cst[x], cre[x].at[i], cssem.at[x], crsem.at[x], device_id=tile_at(o), device_id_type=MESH
-                ).start()
-            cre[x][len(CORNER_OFFS)] = cst[x][...]
+
+    def send(x, stage, land):
+        spread(stage, land, ssem.at[x], rsem.at[x])
         land[len(LINE_OFFS)] = stage[...]
 
-    def receive(x, land, width, near):
+    def send_more(x, stage, more, land):
+        lane = lanes(2, HALF)
+        for k in range(4):
+            pair = stage[k, 0:2, :]
+            cst[x][2 * k : 2 * k + 2, :] = jnp.where(lane < 64, pair[:, :HALF], pair[:, HALF:])
+        for o in CORNER_OFFS:
+            i = CORNER_OFFS.index((-o + 6) % TILES - 6)
+            pltpu.make_async_remote_copy(
+                cst[x], cre[x].at[i], cssem.at[x], crsem.at[x], device_id=tile_at(o), device_id_type=MESH
+            ).start()
+        spread(more, land, msem.at[x], mrsem.at[x])
+        cre[x][len(CORNER_OFFS)] = cst[x][...]
+        land[len(LINE_OFFS)] = more[...]
+
+    def receive(come, land, width, near):
         got = land.at[pl.ds(0, len(LINE_OFFS))]
-        pltpu.make_async_copy(got, got, rsem.at[x]).wait()
+        pltpu.make_async_copy(got, got, come).wait()
         for k in range(4):
             near[k * width : (k + 1) * width, :] = land[line_slot[k], k ^ 1]
         back = (HALF - 1) - lanes(8, HALF)
@@ -157,16 +164,16 @@
                 values[k, e] = jnp.where(place == 1, pair[:, HALF - 1 :], pair[:, :1])
         return values
 
-    def advance(near, width, stage, s, ghosts, outer, terms):
+    def advance(near, more, width, stage, s, ghosts, terms):
         lane = lanes(1, TS)
         out = []
         for k in range(4):
-            line = [near[k * width + j : k * width + j + 1, :] for j in range(2)]
+            line = [near[2 * k + j : 2 * k + j + 1, :] for j in range(2)]
             sums = []
             for j in range(2):
                 low = jnp.where(lane < s, ghosts[k, 0][j : j + 1, :], pltpu.roll(line[j], s, 1))
                 high = jnp.where(lane >= TS - s, ghosts[k, 1][j : j + 1, :], pltpu.roll(line[j], TS - s, 1))
-                beyond = near[k * width + outer + j : k * width + outer + j + 1, :]
+                beyond = more[k * width + j : k * width + j + 1, :]
                 sums.append(low + high + beyond + stage[k, j : j + 1, :])
             start0, start1, k00, k11, k01 = terms(k)
             out.append(
@@ -186,8 +193,8 @@
                 hs[j, HALF - 1 - i : HALF - i, :] = lines[3][j]
             hc[j] = jnp.transpose(hs[j])
 
-    def plain_lines(near, width):
-        return [[near[k * width + j : k * width + j + 1, :] for j in range(2)] for k in range(4)]
+    def plain_lines(near):
+        return [[near[2 * k + j : 2 * k + j + 1, :] for j in range(2)] for k in range(4)]
 
     def beside(v, j, r, s):
         lane = lanes(CHUNK, TS)
@@ -210,26 +217,27 @@
             out = jnp.where(lane == HALF - 7 - i, pltpu.roll(x[:, HALF:], HALF - 6 - i, 1), out)
         ec[pl.ds(r, CHUNK), :] = out
 
-    def fill_stage(stage, v, s, second, terms):
+    def fill_stage(stage, v):
         ect[...] = jnp.transpose(ec[...])
         for j in range(2):
             stage[0, j : j + 1, :] = v[j, 8:9, :]
             stage[1, j : j + 1, :] = v[j, 263:264, :]
             stage[2, j : j + 1, :] = ect[3 * j : 3 * j + 1, :]
             stage[3, j : j + 1, :] = ect[127 - 3 * j : 128 - 3 * j, :]
-            if second is not None:
-                b = second + j
-                stage[0, b : b + 1, :] = v[j, 8 + s : 9 + s, :]
-                stage[1, b : b + 1, :] = v[j, 263 - s : 264 - s, :]
-                stage[2, b : b + 1, :] = ect[3 * j + s : 3 * j + s + 1, :]
-                stage[3, b : b + 1, :] = ect[127 - 3 * j - s : 128 - 3 * j - s, :]
+
+    def fill_more(more, v, s, terms):
+        for j in range(2):
+            more[0, j : j + 1, :] = v[j, 8 + s : 9 + s, :]
+            more[1, j : j + 1, :] = v[j, 263 - s : 264 - s, :]
+            more[2, j : j + 1, :] = ect[3 * j + s : 3 * j + s + 1, :]
+            more[3, j : j + 1, :] = ect[127 - 3 * j - s : 128 - 3 * j - s, :]
         if terms is not None:
             for i in range(3):
-                stage[0, 2 + i : 3 + i, :] = terms[i, 0:1, :]
-                stage[1, 2 + i : 3 + i, :] = terms[i, TS - 1 : TS, :]
-                stage[2, 2 + i : 3 + i, :] = ect[6 + i : 7 + i, :]
-                stage[3, 2 + i : 3 + i, :] = ect[121 - i : 122 - i, :]
-            stage[:, 7:8, :] = jnp.zeros((4, 1, TS), jnp.float32)
+                more[0, 2 + i : 3 + i, :] = terms[i, 0:1, :]
+                more[1, 2 + i : 3 + i, :] = terms[i, TS - 1 : TS, :]
+                more[2, 2 + i : 3 + i, :] = ect[6 + i : 7 + i, :]
+                more[3, 2 + i : 3 + i, :] = ect[121 - i : 122 - i, :]
+            more[:, 5:6, :] = jnp.zeros((4, 1, TS), jnp.float32)
 
     def over_chunks(step, first=0, count=CHUNKS):
         def body(i, carry):
@@ -274,10 +282,12 @@
         put_edges(r, q, u, (k00, k11, k01))
 
     over_chunks(start_fine)
-    fill_stage(st1, va, 1, 5, kf)
-    send(0, st1, re1, 8)
-    receive(0, re1, 8, nb1)
-    set_halo(va, 1, plain_lines(nb1, 8))
+    fill_stage(st1, va)
+    send(0, st1, re1)
+    fill_more(mo1, va, 1, kf)
+    send_more(0, st1, mo1, mr1)
+    receive(rsem.at[0], re1, 2, nb1)
+    set_halo(va, 1, plain_lines(nb1))
 
     def first_sweep(r):
         q, u = sweep(va, sf, kf, 1, r)
@@ -285,12 +295,14 @@
 
     over_chunks(first_sweep)
 
-    def terms_of(near):
+    def terms_of(near, more):
         def terms(k):
-            return [near[k * 8 + j : k * 8 + j + 1, :] for j in (0, 1, 2, 3, 4)]
+            starts = [near[2 * k + j : 2 * k + j + 1, :] for j in range(2)]
+            return starts + [more[6 * k + j : 6 * k + j + 1, :] for j in (2, 3, 4)]
         return terms
 
-    set_halo(vb, 1, advance(nb1, 8, st1, 1, corners(0), 5, terms_of(nb1)))
+    receive(mrsem.at[0], mr1, 6, nm1)
+    set_halo(vb, 1, advance(nb1, nm1, 6, st1, 1, corners(0), terms_of(nb1, nm1)))
 
     def start_coarse(r):
         here = pl.ds(r, CHUNK)
@@ -308,17 +320,20 @@
         put_edges(r, q, u, (k00, k11, k01))
 
     over_chunks(start_coarse)
-    fill_stage(st2, ca, 2, 5, kc)
-    send(1, st2, re2, 8)
-    receive(1, re2, 8, nb2)
-    set_halo(ca, 2, plain_lines(nb2, 8))
+    fill_stage(st2, ca)
+    send(1, st2, re2)
+    fill_more(mo2, ca, 2, kc)
+    send_more(1, st2, mo2, mr2)
+    receive(rsem.at[1], re2, 2, nb2)
+    set_halo(ca, 2, plain_lines(nb2))
 
     def coarse_sweep(r):
         q, u = sweep(ca, sc, kc, 2, r)
         cb[0, pl.ds(r + 8, CHUNK), :], cb[1, pl.ds(r + 8, CHUNK), :] = q, u
 
     over_chunks(coarse_sweep)
-    set_halo(cb, 2, advance(nb2, 8, st2, 2, corners(1), 5, terms_of(nb2)))
+    receive(mrsem.at[1], mr2, 6, nm2)
+    set_halo(cb, 2, advance(nb2, nm2, 6, st2, 2, corners(1), terms_of(nb2, nm2)))
 
     def correct(r):
         q, u = sweep(cb, sc, kc, 2, r)
@@ -329,12 +344,15 @@
         put_edges(r, q, u)
 
     over_chunks(correct)
-    fill_stage(st3, va, 1, 2, None)
-    send(2, st3, re3, 4)
-    receive(2, re3, 4, nb3)
-    set_halo(va, 1, plain_lines(nb3, 4))
+    fill_stage(st3, va)
+    send(2, st3, re3)
+    fill_more(mo3, va, 1, None)
+    send_more(2, st3, mo3, mr3)
+    receive(rsem.at[2], re3, 2, nb3)
+    set_halo(va, 1, plain_lines(nb3))
     over_chunks(first_sweep)
-    set_halo(vb, 1, advance(nb3, 4, st3, 1, corners(2), 2, terms_of(nb1)))
+    receive(mrsem.at[2], mr3, 2, nm3)
+    set_halo(vb, 1, advance(nb3, nm3, 2, st3, 1, corners(2), terms_of(nb1, nm1)))
 
     def last_sweep(r):
         q, u = sweep(vb, sf, kf, 1, r)
@@ -342,10 +360,10 @@
         put_edges(r, q, u)
 
     over_chunks(last_sweep)
-    fill_stage(st4, va, 1, None, None)
-    send(3, st4, re4, 2)
-    receive(3, re4, 2, nb4)
-    set_halo(va, 1, plain_lines(nb4, 2))
+    fill_stage(st4, va)
+    send(3, st4, re4)
+    receive(rsem.at[3], re4, 2, nb4)
+    set_halo(va, 1, plain_lines(nb4))
 
     def finish(i):
         r = pl.multiple_of(band + i, CHUNK)
@@ -362,6 +380,8 @@
         if x < 3:
             sent = cre[x].at[pl.ds(0, len(CORNER_OFFS))]
             pltpu.make_async_copy(sent, sent, cssem.at[x]).wait()
+            sent = (mr1, mr2, mr3)[x].at[pl.ds(0, len(LINE_OFFS))]
+            pltpu.make_async_copy(sent, sent, msem.at[x]).wait()
 
 
 def body(right_side, pixel_weight, noise_diag, noise_corr, neighbours):
@@ -369,7 +389,7 @@
     vm = pltpu.VMEM
     plane, pair, triple, padded = (TS, TS), (2, TS, TS), (3, TS, TS), (2, TS + 16, TS)
     hbm = pl.BlockSpec(memory_space=pl.ANY)
-    widths = (8, 8, 4, 2)
+    widths, later = (2, 2, 2, 2), (6, 6, 2)
     dma = pltpu.SemaphoreType.DMA
     return pl.pallas_call(
         kernel,
@@ -387,7 +407,10 @@
         + [vm((4 * n, TS), f32) for n in widths]
         + [
             *[vm((8, HALF), f32)] * 3, *[vm((26, 8, HALF), f32)] * 3,
-            dma((6,)), dma((6,)), dma((6,)), dma((4,)), dma((4,)), dma((3,)), dma((3,)),
+            *[vm((4, n, TS), f32) for n in later],
+            *[vm((14, 4, n, TS), f32) for n in later],
+            *[vm((4 * n, TS), f32) for n in later],
+            dma((6,)), dma((6,)), dma((6,)), dma((4,)), dma((4,)), dma((3,)), dma((3,)), dma((3,)), dma((3,)),
         ],
         compiler_params=pltpu.CompilerParams(
             collective_id=0, has_side_effects=True, vmem_limit_bytes=48 * 2**20

time: 64.5 us -> 65.8 us (1.020)
  Pallas kernels: 57.8 us -> 59.1 us
    pallas_call x1, Pallas kernels: 57.8 us -> 59.1 us  [body(): pl.pallas_call(kernel, out_shape=[jax.ShapeDtypeStruct((2, HALF, TS), f32...]
where the time goes in v3:
time: 65.8 us; the launch traced here: 65.6 us
  Pallas kernels  59.1 us (90%)
  local copies, waits for them, and re-layouts  5.8 us (9%)
    pallas_call x1, Pallas kernels, body(): pl.pallas_call(kernel, out_shape=[jax.ShapeDtypeStruct((2, HALF, TS), f32...  59.1 us
    unnamed x12, local copies, waits for them, and re-layouts  5.8 us

profile of v3, /device:TPU:2, one launch (start us, length us, event | category | flops | bytes accessed | tf_op | source)
XLA Modules:
  0.0 65.6 jit_solution(10636292458695110819)
XLA Ops:
  0.6 0.0 copy-start
  0.6 0.9 %copy-done = f32[2,128,256]{2,1,0:T(8,128)S(1)} copy-done((f32[2,128,256]{2,1,0:T(8,128)S(1)}, f32[2,128,256]{2,1,0:T(8,128)}, u32[]{:S(2)}) %copy-start) | copy-done | bytes 262168
  1.6 0.0 copy-start.1
  1.6 0.9 %copy-done.1 = f32[2,128,256]{2,1,0:T(8,128)S(1)} copy-done((f32[2,128,256]{2,1,0:T(8,128)S(1)}, f32[2,128,256]{2,1,0:T(8,128)}, u32[]{:S(2)}) %copy-start.1) | copy-done | bytes 262168
  2.5 0.0 copy-start.2
  2.5 0.9 %copy-done.2 = f32[128,256]{1,0:T(8,128)S(1)} copy-done((f32[128,256]{1,0:T(8,128)S(1)}, f32[128,256]{1,0:T(8,128)}, u32[]{:S(2)}) %copy-start.2) | copy-done | bytes 131096
  3.4 0.0 copy-start.3
  3.4 0.9 %copy-done.3 = f32[128,256]{1,0:T(8,128)S(1)} copy-done((f32[128,256]{1,0:T(8,128)S(1)}, f32[128,256]{1,0:T(8,128)}, u32[]{:S(2)}) %copy-start.3) | copy-done | bytes 131096
  4.3 0.0 copy-start.4
  4.3 0.7 %copy-done.4 = s32[3,4,128]{2,1,0:T(4,128)S(1)} copy-done((s32[3,4,128]{2,1,0:T(4,128)S(1)}, s32[3,4,128]{2,1,0:T(4,128)}, u32[]{:S(2)}) %copy-start.4) | copy-done | bytes 6168
  5.0 59.1 %shard_map.68 = (f32[2,128,256]{2,1,0:T(8,128)S(1)}, f32[2,128,256]{2,1,0:T(8,128)S(1)}) custom-call(s32[3,4,128]{2,1,0:T(4,128)S(1)} %copy-done.4, f32[2,128,256]{2,1,0:T(8,128)S(1)} %copy-done, f32[128,256]{1,0:T(8,128)S(1)} %copy-done.2, f32[2,128,256]{2,1,0:T(8,128)S(1)} %copy-done.1, f32[128,256]{1,0:T(8,128)S(1)} %copy-done.3), custom_call_target="tpu_custom_call" | custom-call | tf_op jit(solution)/shard_map/pallas_call | solution.py:394
  64.2 0.7 %copy.9 = f32[2,128,256]{2,1,0:T(8,128)} copy(f32[2,128,256]{2,1,0:T(8,128)S(1)} %get-tuple-element.4) | data formatting | bytes 524288
  64.9 0.7 %copy.10 = f32[2,128,256]{2,1,0:T(8,128)} copy(f32[2,128,256]{2,1,0:T(8,128)S(1)} %get-tuple-element.5) | data formatting | bytes 524288
Async XLA Ops:
  0.6 1.0 %copy-start = (f32[2,128,256]{2,1,0:T(8,128)S(1)}, f32[2,128,256]{2,1,0:T(8,128)}, u32[]{:S(2)}) copy-start(f32[2,128,256]{2,1,0:T(8,128)} %rs_in.1) | copy-start | bytes 786436
  1.6 0.9 %copy-start.1 = (f32[2,128,256]{2,1,0:T(8,128)S(1)}, f32[2,128,256]{2,1,0:T(8,128)}, u32[]{:S(2)}) copy-start(f32[2,128,256]{2,1,0:T(8,128)} %nd_in.1) | copy-start | bytes 786436
  2.5 0.9 %copy-start.2 = (f32[128,256]{1,0:T(8,128)S(1)}, f32[128,256]{1,0:T(8,128)}, u32[]{:S(2)}) copy-start(f32[128,256]{1,0:T(8,128)} %w_in.1) | copy-start | bytes 393220
  3.4 0.9 %copy-start.3 = (f32[128,256]{1,0:T(8,128)S(1)}, f32[128,256]{1,0:T(8,128)}, u32[]{:S(2)}) copy-start(f32[128,256]{1,0:T(8,128)} %nc_in.1) | copy-start | bytes 393220
  4.3 0.7 %copy-start.4 = (s32[3,4,128]{2,1,0:T(4,128)S(1)}, s32[3,4,128]{2,1,0:T(4,128)}, u32[]{:S(2)}) copy-start(s32[3,4,128]{2,1,0:T(4,128)} %nb.1) | copy-start | bytes 18436

commit v4 on v2

--- a/solution.py
+++ b/solution.py
@@ -16,7 +16,7 @@
 TILES = 128
 CHUNK = 8
 CHUNKS = TS // CHUNK
-BATCH = 4
+BATCH = 8
 MESH = pl.DeviceIdType.MESH
 
 LINE_OFFS = [-3, -2, -1, 1, 2, 3] + [64 + d for d in range(-3, 4)]
@@ -258,7 +258,7 @@
         return mq, mu, q0, u0
 
     hs[...] = jnp.zeros_like(hs)
-    for m in local + shared:
+    for m in local:
         m.wait()
 
     def start_fine(r):
@@ -273,7 +273,10 @@
         va[0, pl.ds(r + 8, CHUNK), :], va[1, pl.ds(r + 8, CHUNK), :] = q, u
         put_edges(r, q, u, (k00, k11, k01))
 
-    over_chunks(start_fine)
+    over_chunks(start_fine, band, CHUNKS // 2)
+    for m in shared:
+        m.wait()
+    over_chunks(start_fine, pl.multiple_of(HALF - band, HALF), CHUNKS // 2)
     fill_stage(st1, va, 1, 5, kf)
     send(0, st1, re1, 8)
     receive(0, re1, 8, nb1)

time: 64.5 us -> 62.5 us (0.969)
  Pallas kernels: 57.8 us -> 55.8 us
    pallas_call x1, Pallas kernels: 57.8 us -> 55.8 us  [body(): pl.pallas_call(kernel, out_shape=[jax.ShapeDtypeStruct((2, HALF, TS), f32...]
where the time goes in v4:
time: 62.5 us; the launch traced here: 62.2 us
  Pallas kernels  55.8 us (89%)
  local copies, waits for them, and re-layouts  5.8 us (9%)
  between operations  0.65 us (1%)
    pallas_call x1, Pallas kernels, body(): pl.pallas_call(kernel, out_shape=[jax.ShapeDtypeStruct((2, HALF, TS), f32...  55.8 us
    unnamed x12, local copies, waits for them, and re-layouts  5.8 us

profile of v4, /device:TPU:2, one launch (start us, length us, event | category | flops | bytes accessed | tf_op | source)
XLA Modules:
  0.0 62.2 jit_solution(16302894870026127346)
XLA Ops:
  0.6 0.0 copy-start
  0.6 0.9 %copy-done = f32[2,128,256]{2,1,0:T(8,128)S(1)} copy-done((f32[2,128,256]{2,1,0:T(8,128)S(1)}, f32[2,128,256]{2,1,0:T(8,128)}, u32[]{:S(2)}) %copy-start) | copy-done | bytes 262168
  1.6 0.0 copy-start.1
  1.6 0.9 %copy-done.1 = f32[2,128,256]{2,1,0:T(8,128)S(1)} copy-done((f32[2,128,256]{2,1,0:T(8,128)S(1)}, f32[2,128,256]{2,1,0:T(8,128)}, u32[]{:S(2)}) %copy-start.1) | copy-done | bytes 262168
  2.5 0.0 copy-start.2
  2.5 0.9 %copy-done.2 = f32[128,256]{1,0:T(8,128)S(1)} copy-done((f32[128,256]{1,0:T(8,128)S(1)}, f32[128,256]{1,0:T(8,128)}, u32[]{:S(2)}) %copy-start.2) | copy-done | bytes 131096
  3.4 0.0 copy-start.3
  3.4 0.9 %copy-done.3 = f32[128,256]{1,0:T(8,128)S(1)} copy-done((f32[128,256]{1,0:T(8,128)S(1)}, f32[128,256]{1,0:T(8,128)}, u32[]{:S(2)}) %copy-start.3) | copy-done | bytes 131096
  4.3 0.0 copy-start.4
  4.3 0.7 %copy-done.4 = s32[3,4,128]{2,1,0:T(4,128)S(1)} copy-done((s32[3,4,128]{2,1,0:T(4,128)S(1)}, s32[3,4,128]{2,1,0:T(4,128)}, u32[]{:S(2)}) %copy-start.4) | copy-done | bytes 6168
  5.0 55.8 %shard_map.68 = (f32[2,128,256]{2,1,0:T(8,128)S(1)}, f32[2,128,256]{2,1,0:T(8,128)S(1)}) custom-call(s32[3,4,128]{2,1,0:T(4,128)S(1)} %copy-done.4, f32[2,128,256]{2,1,0:T(8,128)S(1)} %copy-done, f32[128,256]{1,0:T(8,128)S(1)} %copy-done.2, f32[2,128,256]{2,1,0:T(8,128)S(1)} %copy-done.1, f32[128,256]{1,0:T(8,128)S(1)} %copy-done.3), custom_call_target="tpu_custom_call" | custom-call | tf_op jit(solution)/shard_map/pallas_call | solution.py:377
  60.8 0.7 %copy.9 = f32[2,128,256]{2,1,0:T(8,128)} copy(f32[2,128,256]{2,1,0:T(8,128)S(1)} %get-tuple-element.4) | data formatting | bytes 524288
  61.5 0.7 %copy.10 = f32[2,128,256]{2,1,0:T(8,128)} copy(f32[2,128,256]{2,1,0:T(8,128)S(1)} %get-tuple-element.5) | data formatting | bytes 524288
Async XLA Ops:
  0.6 1.0 %copy-start = (f32[2,128,256]{2,1,0:T(8,128)S(1)}, f32[2,128,256]{2,1,0:T(8,128)}, u32[]{:S(2)}) copy-start(f32[2,128,256]{2,1,0:T(8,128)} %rs_in.1) | copy-start | bytes 786436
  1.6 0.9 %copy-start.1 = (f32[2,128,256]{2,1,0:T(8,128)S(1)}, f32[2,128,256]{2,1,0:T(8,128)}, u32[]{:S(2)}) copy-start(f32[2,128,256]{2,1,0:T(8,128)} %nd_in.1) | copy-start | bytes 786436
  2.5 0.9 %copy-start.2 = (f32[128,256]{1,0:T(8,128)S(1)}, f32[128,256]{1,0:T(8,128)}, u32[]{:S(2)}) copy-start(f32[128,256]{1,0:T(8,128)} %w_in.1) | copy-start | bytes 393220
  3.4 0.9 %copy-start.3 = (f32[128,256]{1,0:T(8,128)S(1)}, f32[128,256]{1,0:T(8,128)}, u32[]{:S(2)}) copy-start(f32[128,256]{1,0:T(8,128)} %nc_in.1) | copy-start | bytes 393220
  4.3 0.7 %copy-start.4 = (s32[3,4,128]{2,1,0:T(4,128)S(1)}, s32[3,4,128]{2,1,0:T(4,128)}, u32[]{:S(2)}) copy-start(s32[3,4,128]{2,1,0:T(4,128)} %nb.1) | copy-start | bytes 18436

commit v5 on v4

--- a/solution.py
+++ b/solution.py
@@ -43,20 +43,17 @@
     return x + jnp.where(row % 2 == 0, pltpu.roll(x, CHUNK - 1, 0), pltpu.roll(x, 1, 0))
 
 
-def smoother_terms(stiffness, w, n0, n1, cross, f0, f1):
-    diag = (stiffness * CENTRE) * w * w
+def smoother_terms(stiffness, w, n0, n1, cross):
+    ww = stiffness * w * w
+    diag = CENTRE * ww
     b00, b11 = diag + n0, diag + n1
-    scale = OMEGA / (b00 * b11 - cross * cross)
-    k00, k11, k01 = scale * b11, scale * b00, -(scale * cross)
-    v0 = w * (k00 * f0 + k01 * f1)
-    v1 = w * (k01 * f0 + k11 * f1)
-    ww = stiffness * w * w
-    return v0, v1, ww * k00, ww * k11, ww * k01
+    scale = ww * (OMEGA / (b00 * b11 - cross * cross))
+    return scale * b11, scale * b00, -(scale * cross)
 
 
 def kernel(
     nb, rs_in, w_in, nd_in, nc_in, sol_out, mis_out,
-    rs, wt, nd, nc, iw, kf, kc, sf, sc, wiw, va, vb, ca, cb,
+    rs, wt, nd, nc, iw, kf, kc, sf, sc, wiw, icw, va, vb, ca, cb,
     ec, ect, hs, hc, st1, st2, st3, st4, re1, re2, re3, re4, nb1, nb2, nb3, nb4,
     cs1, cs2, cs3, cr1, cr2, cr3, lsem, psem, prem, ssem, rsem, cssem, crsem,
 ):
@@ -266,8 +263,11 @@
         n0, n1, w = nd[0, here, :], nd[1, here, :], wt[here, :]
         cross = nc[here, :] * jnp.sqrt(n0 * n1)
         nc[here, :] = cross
-        iw[here, :] = 1.0 / w
-        q, u, k00, k11, k01 = smoother_terms(1.0, w, n0, n1, cross, rs[0, here, :], rs[1, here, :])
+        inv = 1.0 / w
+        iw[here, :] = inv
+        k00, k11, k01 = smoother_terms(1.0, w, n0, n1, cross)
+        f0, f1 = rs[0, here, :] * inv, rs[1, here, :] * inv
+        q, u = k00 * f0 + k01 * f1, k01 * f0 + k11 * f1
         kf[0, here, :], kf[1, here, :], kf[2, here, :] = k00, k11, k01
         sf[0, here, :], sf[1, here, :] = q, u
         va[0, pl.ds(r + 8, CHUNK), :], va[1, pl.ds(r + 8, CHUNK), :] = q, u
@@ -279,6 +279,18 @@
     over_chunks(start_fine, pl.multiple_of(HALF - band, HALF), CHUNKS // 2)
     fill_stage(st1, va, 1, 5, kf)
     send(0, st1, re1, 8)
+
+    def coarse_terms(r):
+        here = pl.ds(r, CHUNK)
+        w = wt[here, :]
+        cw = 0.25 * pair_sum(w)
+        icw[here, :] = 0.5 / cw
+        wiw[here, :] = w / cw
+        kc[0, here, :], kc[1, here, :], kc[2, here, :] = smoother_terms(
+            2.0, cw, pair_sum(nd[0, here, :]), pair_sum(nd[1, here, :]), pair_sum(nc[here, :])
+        )
+
+    over_chunks(coarse_terms)
     receive(0, re1, 8, nb1)
     set_halo(va, 1, plain_lines(nb1, 8))
 
@@ -298,14 +310,10 @@
     def start_coarse(r):
         here = pl.ds(r, CHUNK)
         mq, mu, _, _ = residual(vb, r)
-        w = wt[here, :]
-        cw = 0.25 * pair_sum(w)
-        wiw[here, :] = w / cw
-        q, u, k00, k11, k01 = smoother_terms(
-            2.0, cw, pair_sum(nd[0, here, :]), pair_sum(nd[1, here, :]), pair_sum(nc[here, :]),
-            pair_sum(mq), pair_sum(mu),
-        )
-        kc[0, here, :], kc[1, here, :], kc[2, here, :] = k00, k11, k01
+        inv = icw[here, :]
+        f0, f1 = pair_sum(mq) * inv, pair_sum(mu) * inv
+        k00, k11, k01 = kc[0, here, :], kc[1, here, :], kc[2, here, :]
+        q, u = k00 * f0 + k01 * f1, k01 * f0 + k11 * f1
         sc[0, here, :], sc[1, here, :] = q, u
         ca[0, pl.ds(r + 8, CHUNK), :], ca[1, pl.ds(r + 8, CHUNK), :] = q, u
         put_edges(r, q, u, (k00, k11, k01))
@@ -381,7 +389,7 @@
         out_specs=[pl.BlockSpec(memory_space=pltpu.VMEM)] * 2,
         scratch_shapes=[
             vm(pair, f32), vm(plane, f32), vm(pair, f32), vm(plane, f32), vm(plane, f32),
-            vm(triple, f32), vm(triple, f32), vm(pair, f32), vm(pair, f32), vm(plane, f32),
+            vm(triple, f32), vm(triple, f32), vm(pair, f32), vm(pair, f32), vm(plane, f32), vm(plane, f32),
             vm(padded, f32), vm(padded, f32), vm(padded, f32), vm(padded, f32),
             vm((TS, HALF), f32), vm((HALF, TS), f32), vm((2, HALF, TS), f32), vm((2, TS, HALF), f32),
         ]

time: 62.5 us -> 60.7 us (0.971)
  Pallas kernels: 55.8 us -> 54 us
    pallas_call x1, Pallas kernels: 55.8 us -> 54 us  [body(): pl.pallas_call(kernel, out_shape=[jax.ShapeDtypeStruct((2, HALF, TS), f32...]
where the time goes in v5:
time: 60.7 us; the launch traced here: 60.5 us
  Pallas kernels  54 us (89%)
  local copies, waits for them, and re-layouts  5.8 us (10%)
  between operations  0.65 us (1%)
    pallas_call x1, Pallas kernels, body(): pl.pallas_call(kernel, out_shape=[jax.ShapeDtypeStruct((2, HALF, TS), f32...  54 us
    unnamed x12, local copies, waits for them, and re-layouts  5.8 us

profile of v5, /device:TPU:2, one launch (start us, length us, event | category | flops | bytes accessed | tf_op | source)
XLA Modules:
  0.0 60.5 jit_solution(7994844758113768188)
XLA Ops:
  0.6 0.0 copy-start
  0.6 0.9 %copy-done = f32[2,128,256]{2,1,0:T(8,128)S(1)} copy-done((f32[2,128,256]{2,1,0:T(8,128)S(1)}, f32[2,128,256]{2,1,0:T(8,128)}, u32[]{:S(2)}) %copy-start) | copy-done | bytes 262168
  1.6 0.0 copy-start.1
  1.6 0.9 %copy-done.1 = f32[2,128,256]{2,1,0:T(8,128)S(1)} copy-done((f32[2,128,256]{2,1,0:T(8,128)S(1)}, f32[2,128,256]{2,1,0:T(8,128)}, u32[]{:S(2)}) %copy-start.1) | copy-done | bytes 262168
  2.5 0.0 copy-start.2
  2.5 0.9 %copy-done.2 = f32[128,256]{1,0:T(8,128)S(1)} copy-done((f32[128,256]{1,0:T(8,128)S(1)}, f32[128,256]{1,0:T(8,128)}, u32[]{:S(2)}) %copy-start.2) | copy-done | bytes 131096
  3.4 0.0 copy-start.3
  3.4 0.9 %copy-done.3 = f32[128,256]{1,0:T(8,128)S(1)} copy-done((f32[128,256]{1,0:T(8,128)S(1)}, f32[128,256]{1,0:T(8,128)}, u32[]{:S(2)}) %copy-start.3) | copy-done | bytes 131096
  4.3 0.0 copy-start.4
  4.3 0.7 %copy-done.4 = s32[3,4,128]{2,1,0:T(4,128)S(1)} copy-done((s32[3,4,128]{2,1,0:T(4,128)S(1)}, s32[3,4,128]{2,1,0:T(4,128)}, u32[]{:S(2)}) %copy-start.4) | copy-done | bytes 6168
  5.0 54.0 %shard_map.68 = (f32[2,128,256]{2,1,0:T(8,128)S(1)}, f32[2,128,256]{2,1,0:T(8,128)S(1)}) custom-call(s32[3,4,128]{2,1,0:T(4,128)S(1)} %copy-done.4, f32[2,128,256]{2,1,0:T(8,128)S(1)} %copy-done, f32[128,256]{1,0:T(8,128)S(1)} %copy-done.2, f32[2,128,256]{2,1,0:T(8,128)S(1)} %copy-done.1, f32[128,256]{1,0:T(8,128)S(1)} %copy-done.3), custom_call_target="tpu_custom_call" | custom-call | tf_op jit(solution)/shard_map/pallas_call | solution.py:385
  59.1 0.7 %copy.9 = f32[2,128,256]{2,1,0:T(8,128)} copy(f32[2,128,256]{2,1,0:T(8,128)S(1)} %get-tuple-element.4) | data formatting | bytes 524288
  59.8 0.7 %copy.10 = f32[2,128,256]{2,1,0:T(8,128)} copy(f32[2,128,256]{2,1,0:T(8,128)S(1)} %get-tuple-element.5) | data formatting | bytes 524288
Async XLA Ops:
  0.6 1.0 %copy-start = (f32[2,128,256]{2,1,0:T(8,128)S(1)}, f32[2,128,256]{2,1,0:T(8,128)}, u32[]{:S(2)}) copy-start(f32[2,128,256]{2,1,0:T(8,128)} %rs_in.1) | copy-start | bytes 786436
  1.6 0.9 %copy-start.1 = (f32[2,128,256]{2,1,0:T(8,128)S(1)}, f32[2,128,256]{2,1,0:T(8,128)}, u32[]{:S(2)}) copy-start(f32[2,128,256]{2,1,0:T(8,128)} %nd_in.1) | copy-start | bytes 786436
  2.5 0.9 %copy-start.2 = (f32[128,256]{1,0:T(8,128)S(1)}, f32[128,256]{1,0:T(8,128)}, u32[]{:S(2)}) copy-start(f32[128,256]{1,0:T(8,128)} %w_in.1) | copy-start | bytes 393220
  3.4 0.9 %copy-start.3 = (f32[128,256]{1,0:T(8,128)S(1)}, f32[128,256]{1,0:T(8,128)}, u32[]{:S(2)}) copy-start(f32[128,256]{1,0:T(8,128)} %nc_in.1) | copy-start | bytes 393220
  4.3 0.7 %copy-start.4 = (s32[3,4,128]{2,1,0:T(4,128)S(1)}, s32[3,4,128]{2,1,0:T(4,128)}, u32[]{:S(2)}) copy-start(s32[3,4,128]{2,1,0:T(4,128)} %nb.1) | copy-start | bytes 18436
